TPU v7x, 32 devices: a whole 2x2x4 slice. The times are simulated.
32 devices in a mesh: grp: 8 (over y, x, core), seq: 4 (over z).
Axes of the slice: x: 2, y: 2, z: 4, core: 2. Of those that a mesh axis runs over, the one named last changes fastest.
Arguments:
- tokens: bfloat16 [8192, 2048], P(('grp', 'seq')), may hold values from -6 to 6
- cotangent: bfloat16 [8192, 2048], P(('grp', 'seq')), may hold values from -6 to 6
- segment_ids: int32 [8192], P(('grp', 'seq')), may hold values from 0 to 31, never falling along the last dimension, each value on 1 to 768 neighbouring positions
- tile_owner_slots: int32 [166], replicated, may hold values from 0 to 167, as said below
- weights_low: bfloat16 [168, 2048, 128], P('grp', 'seq')
- master: float32 [168, 2048, 128], P('grp', 'seq')
- moment_one: float32 [168, 2048, 128], P('grp', 'seq')
- moment_two: float32 [168, 2048, 128], P('grp', 'seq'), as said below
- left_basis_set: float32 [168, 2048, 512], P('grp', 'seq'), as said below
- right_basis_set: float32 [168, 512, 128], P('grp', 'seq'), as said below
- gains: float32 [2, 2048], replicated, may hold values from 0.5 to 1.5
- gain_moment_one: float32 [2, 2048], replicated, may hold values from -28 to 28
- gain_moment_two: float32 [2, 2048], replicated, may hold values from 430.8992 to 1720.32
Outputs:
- block_out: bfloat16 [8192, 2048], P(('grp', 'seq'))
- input_grad: float32 [8192, 2048], P(('grp', 'seq'))
- new_master: float32 [168, 2048, 128], P('grp', 'seq')
- new_moment_one: float32 [168, 2048, 128], P('grp', 'seq')
- new_moment_two: float32 [168, 2048, 128], P('grp', 'seq')
- gain_grads: float32 [2, 2048], replicated
- new_gains: float32 [2, 2048], replicated
- new_gain_one: float32 [2, 2048], replicated
- new_gain_two: float32 [2, 2048], replicated
Inputs may be any that keep to these rules, and one draw needn't show every extreme that they name: `tile_owner_slots`: the entries are distinct; slot q belongs to data group q // 21. `segment_ids`: never falls along the tokens. `left_basis_set`: each 512 x 512 block is orthogonal. `right_basis_set`: each 128 x 128 block is orthogonal. `moment_two`: positive.
All inputs are finite; a program needn't handle non-finite values.
Results may differ from a plain program's by a relative error of at most 0.015.
Values may be sent and summed in bfloat16 or wider, within the bound.
A program may use at most 704 MiB of HBM per device.

v0:
```python
import jax
import jax.numpy as jnp
from jax import lax
from jax.sharding import PartitionSpec as P

MODEL_WIDTH = 2048
NH = 16
HD = 128
FF = 5632
SEQLEN = 1024
NORM_EPS = 1e-05
BETA_ONE = 0.95
BETA_TWO = 0.95
ADAM_EPS = 1e-08
WEIGHT_DECAY = 0.01
LEARN_RATE = 0.03
GAIN_RATE = 1.5
ROPE_BASE = 10000.0
MASKED = -1e30
PRECISE = lax.Precision.HIGHEST


def rotate(values, positions, direction):
    head_width = values.shape[-1]
    half_width = head_width // 2
    frequency = ROPE_BASE ** (-(jnp.arange(half_width, dtype=jnp.float32) * 2.0) / head_width)
    angles = positions.astype(jnp.float32)[:, None] * frequency[None, :]
    cosine = jnp.cos(angles)[:, None, :]
    sine_part = (jnp.sin(angles) * direction)[:, None, :]
    leading = values[..., :half_width]
    trailing = values[..., half_width:]
    return jnp.concatenate(
        [leading * cosine - trailing * sine_part, trailing * cosine + leading * sine_part], axis=-1
    )


def visible(query_index, key_index, query_seg, key_seg):
    causal = query_index[:, None] >= key_index[None, :]
    same_seq = query_index[:, None] // SEQLEN == key_index[None, :] // SEQLEN
    same_doc = query_seg[:, None] == key_seg[None, :]
    return causal & same_seq & same_doc


def contract(left_side, right_side):
    return lax.dot_general(
        left_side, right_side, (((0,), (0,)), ((), ())), preferred_element_type=jnp.float32
    )


def times_transpose(left_side, right_side):
    return lax.dot_general(
        left_side, right_side, (((1,), (1,)), ((), ())), preferred_element_type=jnp.float32
    )


def attend(queries, key_rows, value_rows, query_index, query_seg, key_index, key_seg):
    query_total, head_count, head_width = queries.shape
    block_rows = min(512, query_total)
    block_count = query_total // block_rows
    score_scale = head_width ** (-0.5)

    def one_block(inputs):
        block_queries, block_index, block_seg = inputs
        raw_scores = jnp.einsum(
            "qhd,kd->hqk", block_queries, key_rows, preferred_element_type=jnp.float32
        )
        allowed = visible(block_index, key_index, block_seg, key_seg)
        score_matrix = jnp.where(allowed[None], raw_scores * score_scale, MASKED)
        highest = jnp.max(score_matrix, axis=-1, keepdims=True)
        exponent = jnp.exp(score_matrix - highest)
        totals = jnp.sum(exponent, axis=-1, keepdims=True)
        probs_low = (exponent / totals).astype(jnp.bfloat16)
        context = jnp.einsum(
            "hqk,kd->qhd", probs_low, value_rows, preferred_element_type=jnp.float32
        )
        return (context, jnp.transpose((highest + jnp.log(totals))[..., 0]))

    context, log_totals = lax.map(
        one_block,
        (
            queries.reshape(block_count, block_rows, head_count, head_width),
            query_index.reshape(block_count, block_rows),
            query_seg.reshape(block_count, block_rows),
        ),
    )
    return (
        context.reshape(query_total, head_count, head_width),
        log_totals.reshape(query_total, head_count),
    )


def attend_back(
    queries, key_rows, value_rows, grads_low, log_totals, query_index, query_seg, key_index, key_seg
):
    query_total, head_count, head_width = queries.shape
    block_rows = min(512, query_total)
    block_count = query_total // block_rows
    score_scale = head_width ** (-0.5)

    def one_block(running, inputs):
        block_queries, block_grads, block_totals, block_index, block_seg = inputs
        raw_scores = jnp.einsum(
            "qhd,kd->hqk", block_queries, key_rows, preferred_element_type=jnp.float32
        )
        allowed = visible(block_index, key_index, block_seg, key_seg)
        shifted = raw_scores * score_scale - jnp.transpose(block_totals)[:, :, None]
        probs = jnp.where(allowed[None], jnp.exp(shifted), 0.0)
        prob_grad = jnp.einsum(
            "qhd,kd->hqk", block_grads, value_rows, preferred_element_type=jnp.float32
        )
        centre = jnp.sum(probs * prob_grad, axis=-1, keepdims=True)
        score_grad = (probs * (prob_grad - centre) * score_scale).astype(jnp.bfloat16)
        query_part = jnp.einsum(
            "hqk,kd->qhd", score_grad, key_rows, preferred_element_type=jnp.float32
        )
        key_part = running[0] + jnp.einsum(
            "hqk,qhd->kd", score_grad, block_queries, preferred_element_type=jnp.float32
        )
        value_part = running[1] + jnp.einsum(
            "hqk,qhd->kd",
            probs.astype(jnp.bfloat16),
            block_grads,
            preferred_element_type=jnp.float32,
        )
        return ((key_part, value_part), query_part)

    zeros_rows = jnp.zeros(key_rows.shape, jnp.float32)
    (key_grad, value_grad), query_grad = lax.scan(
        one_block,
        (zeros_rows, zeros_rows),
        (
            queries.reshape(block_count, block_rows, head_count, head_width),
            grads_low.reshape(block_count, block_rows, head_count, head_width),
            log_totals.reshape(block_count, block_rows, head_count),
            query_index.reshape(block_count, block_rows),
            query_seg.reshape(block_count, block_rows),
        ),
    )
    return (query_grad.reshape(query_total, head_count, head_width), key_grad, value_grad)


def local(
    tokens,
    cotangent,
    segment_ids,
    tile_owner_slots,
    weights_low,
    master,
    moment_one,
    moment_two,
    left_basis_set,
    right_basis_set,
    gains,
    gain_moment_one,
    gain_moment_two,
):
    grp_count = lax.axis_size("grp")
    seq_count = lax.axis_size("seq")
    grp_here = lax.axis_index("grp")
    rows_here = tokens.shape[0]
    slots_here, rows_block, tile_width = weights_low.shape
    query_cols = NH * HD
    value_end = query_cols + 2 * HD
    output_end = value_end + MODEL_WIDTH
    attn_tiles = output_end // tile_width
    hidden_tiles = FF // tile_width
    share = -(-hidden_tiles // grp_count)
    share_cols = share * tile_width
    sub_rows = rows_block // grp_count
    local_index = lax.axis_index("seq") * rows_here + jnp.arange(rows_here, dtype=jnp.int32)
    local_place = local_index % SEQLEN
    plane_tiles = lax.all_gather(weights_low, "grp", axis=0, tiled=True)
    hidden_ids = grp_here * share + jnp.arange(share, dtype=jnp.int32)
    real = hidden_ids < hidden_tiles
    hidden_ids = jnp.minimum(hidden_ids, hidden_tiles - 1)
    feed_ids = (
        attn_tiles + jnp.arange(3, dtype=jnp.int32)[:, None] * hidden_tiles + hidden_ids[None, :]
    ).reshape(-1)
    attn_rows = lax.dynamic_slice_in_dim(plane_tiles, grp_here * sub_rows, sub_rows, axis=1)
    attn_rows = jnp.transpose(attn_rows[tile_owner_slots[:attn_tiles]], (1, 0, 2)).reshape(
        sub_rows, output_end
    )
    attn_weights = lax.all_gather(attn_rows, "seq", axis=0, tiled=False)
    attn_weights = lax.all_gather(attn_weights, "grp", axis=1, tiled=True).reshape(
        MODEL_WIDTH, output_end
    )
    feed_tiles = jnp.where(
        jnp.tile(real, 3)[:, None, None], plane_tiles[tile_owner_slots[feed_ids]], 0
    )
    feed_rows = jnp.transpose(feed_tiles, (1, 0, 2)).reshape(rows_block, 3 * share_cols)
    feed_weights = lax.all_gather(feed_rows, "seq", axis=0, tiled=True)
    cot_plane = lax.all_gather(cotangent, "grp", axis=0, tiled=True)
    tok_float = tokens.astype(jnp.float32)
    inverse_one = lax.rsqrt(jnp.mean(tok_float * tok_float, axis=-1, keepdims=True) + NORM_EPS)
    normed = (tok_float * inverse_one * gains[0]).astype(jnp.bfloat16)
    projected = jnp.dot(normed, attn_weights[:, :value_end], preferred_element_type=jnp.float32)
    queries = rotate(projected[:, :query_cols].reshape(rows_here, NH, HD), local_place, 1.0).astype(
        jnp.bfloat16
    )
    key_rows = (
        rotate(
            projected[:, query_cols : query_cols + HD].reshape(rows_here, 1, HD), local_place, 1.0
        )
        .reshape(rows_here, HD)
        .astype(jnp.bfloat16)
    )
    value_rows = projected[:, query_cols + HD : value_end].astype(jnp.bfloat16)
    all_pairs = lax.all_gather(
        jnp.concatenate([key_rows, value_rows], axis=1), "seq", axis=0, tiled=True
    )
    all_keys = all_pairs[:, :HD]
    all_values = all_pairs[:, HD:]
    all_segs = lax.all_gather(segment_ids, "seq", axis=0, tiled=True)
    group_index = jnp.arange(all_keys.shape[0], dtype=jnp.int32)
    group_place = group_index % SEQLEN
    heads_here = NH // seq_count
    head_queries = lax.all_to_all(
        queries.reshape(rows_here, query_cols), "seq", split_axis=1, concat_axis=0, tiled=True
    ).reshape(-1, heads_here, HD)
    head_context, log_totals = attend(
        head_queries, all_keys, all_values, group_index, all_segs, group_index, all_segs
    )
    context = lax.all_to_all(
        head_context.reshape(-1, heads_here * HD).astype(jnp.bfloat16),
        "seq",
        split_axis=0,
        concat_axis=1,
        tiled=True,
    )
    branch = jnp.dot(context, attn_weights[:, value_end:], preferred_element_type=jnp.float32)
    hidden = tok_float + branch
    inverse_two = lax.rsqrt(jnp.mean(hidden * hidden, axis=-1, keepdims=True) + NORM_EPS)
    normed_two = (hidden * inverse_two * gains[1]).astype(jnp.bfloat16)
    normed_plane = lax.all_gather(normed_two, "grp", axis=0, tiled=True)
    gating_weights = feed_weights[:, : 2 * share_cols]
    down_weights = feed_weights[:, 2 * share_cols :]
    gate_up = jnp.dot(normed_plane, gating_weights, preferred_element_type=jnp.float32)
    gate = gate_up[:, :share_cols]
    upper = gate_up[:, share_cols:]
    sigmoid_gate = jax.nn.sigmoid(gate)
    silu_gate = jax.nn.silu(gate)
    activated = (silu_gate * upper).astype(jnp.bfloat16)
    act_grad = jnp.dot(cot_plane, down_weights, preferred_element_type=jnp.float32)
    gate_grad = (act_grad * upper * sigmoid_gate * (1.0 + gate * (1.0 - sigmoid_gate))).astype(
        jnp.bfloat16
    )
    up_grad = (act_grad * silu_gate).astype(jnp.bfloat16)
    gating_grad = jnp.concatenate([gate_grad, up_grad], axis=1)
    norm_two_grad = lax.psum_scatter(
        times_transpose(gating_grad, gating_weights).astype(jnp.bfloat16),
        "grp",
        scatter_dimension=0,
        tiled=True,
    ).astype(jnp.float32)
    feed_grads = jnp.concatenate(
        [contract(normed_plane, gating_grad), contract(cot_plane, activated)], axis=1
    ).astype(jnp.bfloat16)
    feed_grads = lax.psum_scatter(feed_grads, "seq", scatter_dimension=0, tiled=True)
    feed_grads = jnp.transpose(feed_grads.reshape(rows_block, 3 * share, tile_width), (1, 0, 2))
    feed_grads = lax.all_gather(feed_grads, "grp", axis=0, tiled=True)
    feed_out = lax.psum_scatter(
        times_transpose(activated, down_weights).astype(jnp.bfloat16),
        "grp",
        scatter_dimension=0,
        tiled=True,
    ).astype(jnp.float32)
    block_out = (hidden + feed_out).astype(jnp.bfloat16)
    out_grad = cotangent.astype(jnp.float32)
    gain_two_term = jnp.sum(norm_two_grad * hidden * inverse_two, axis=0)
    hidden_grad = (
        out_grad
        + inverse_two * gains[1] * norm_two_grad
        - hidden
        * inverse_two**3
        * jnp.mean(hidden * gains[1] * norm_two_grad, axis=-1, keepdims=True)
    )
    branch_grad = hidden_grad.astype(jnp.bfloat16)
    context_grad = times_transpose(branch_grad, attn_weights[:, value_end:]).astype(jnp.bfloat16)
    head_grads = lax.all_to_all(
        context_grad, "seq", split_axis=1, concat_axis=0, tiled=True
    ).reshape(-1, heads_here, HD)

    def reduce_rows(part):
        cols = part.shape[1]
        blocks = jnp.transpose(
            part.astype(jnp.bfloat16).reshape(seq_count, grp_count, sub_rows, cols), (1, 0, 2, 3)
        ).reshape(grp_count * seq_count * sub_rows, cols)
        summed = lax.psum_scatter(blocks, ("grp", "seq"), scatter_dimension=0, tiled=True)
        return lax.all_gather(summed, "grp", axis=0, tiled=True)

    out_grads = reduce_rows(contract(context, branch_grad))
    head_query_grad, key_part, value_part = attend_back(
        head_queries,
        all_keys,
        all_values,
        head_grads,
        log_totals,
        group_index,
        all_segs,
        group_index,
        all_segs,
    )
    turned_query = (
        rotate(head_query_grad, group_place, -1.0).reshape(-1, heads_here * HD).astype(jnp.bfloat16)
    )
    query_grad = lax.all_to_all(turned_query, "seq", split_axis=0, concat_axis=1, tiled=True)
    key_part = rotate(key_part[:, None, :], group_place, -1.0)[:, 0, :]
    pair_grad = lax.psum_scatter(
        jnp.concatenate([key_part, value_part], axis=1), "seq", scatter_dimension=0, tiled=True
    )
    projected_grad = jnp.concatenate([query_grad, pair_grad.astype(jnp.bfloat16)], axis=1)
    in_grads = reduce_rows(contract(normed, projected_grad))
    norm_one_grad = times_transpose(projected_grad, attn_weights[:, :value_end])
    gain_one_term = jnp.sum(norm_one_grad * tok_float * inverse_one, axis=0)
    input_grad = (
        hidden_grad
        + inverse_one * gains[0] * norm_one_grad
        - tok_float
        * inverse_one**3
        * jnp.mean(tok_float * gains[0] * norm_one_grad, axis=-1, keepdims=True)
    )
    gain_grads = lax.psum(jnp.stack([gain_one_term, gain_two_term]), ("grp", "seq"))
    tile_count = tile_owner_slots.shape[0]
    tile_of_slot = (
        jnp.full((grp_count * slots_here,), tile_count, jnp.int32)
        .at[tile_owner_slots]
        .set(jnp.arange(tile_count, dtype=jnp.int32))
    )
    tiles_here = lax.dynamic_slice_in_dim(tile_of_slot, grp_here * slots_here, slots_here)
    attn_grads = jnp.transpose(
        jnp.concatenate([in_grads, out_grads], axis=1).reshape(rows_block, attn_tiles, tile_width),
        (1, 0, 2),
    )
    feed_at = jnp.clip(tiles_here - attn_tiles, 0, 3 * hidden_tiles - 1)
    which, column = (feed_at // hidden_tiles, feed_at % hidden_tiles)
    feed_at = column // share * (3 * share) + which * share + column % share
    picked = jnp.where(
        (tiles_here < attn_tiles)[:, None, None],
        attn_grads[jnp.minimum(tiles_here, attn_tiles - 1)],
        feed_grads[feed_at],
    )
    reduced_sum = jnp.where((tiles_here < tile_count)[:, None, None], picked, 0).astype(jnp.float32)
    turned = jnp.einsum("zji,zjc->zic", left_basis_set, reduced_sum)
    turned = jnp.einsum("zic,zcd->zid", turned, right_basis_set)
    new_one = BETA_ONE * moment_one + (1.0 - BETA_ONE) * turned
    new_two = BETA_TWO * moment_two + (1.0 - BETA_TWO) * turned * turned
    scaled = new_one / (jnp.sqrt(new_two) + ADAM_EPS)
    restored = jnp.einsum("zij,zjd->zid", left_basis_set, scaled)
    restored = jnp.einsum("zid,zed->zie", restored, right_basis_set)
    new_master = master * (1.0 - LEARN_RATE * WEIGHT_DECAY) - LEARN_RATE * restored
    gain_one = BETA_ONE * gain_moment_one + (1.0 - BETA_ONE) * gain_grads
    gain_two = BETA_TWO * gain_moment_two + (1.0 - BETA_TWO) * gain_grads * gain_grads
    new_gains = gains - GAIN_RATE * gain_one / (jnp.sqrt(gain_two) + ADAM_EPS)
    return (
        block_out,
        input_grad,
        new_master,
        new_one,
        new_two,
        gain_grads,
        new_gains,
        gain_one,
        gain_two,
    )


def solution(mesh):
    return jax.shard_map(
        local,
        mesh=mesh,
        in_specs=(
            P(("grp", "seq"), None),
            P(("grp", "seq"), None),
            P(("grp", "seq")),
            P(),
            P("grp", "seq", None),
            P("grp", "seq", None),
            P("grp", "seq", None),
            P("grp", "seq", None),
            P("grp", "seq", None),
            P("grp", "seq", None),
            P(),
            P(),
            P(),
        ),
        out_specs=(
            P(("grp", "seq"), None),
            P(("grp", "seq"), None),
            P("grp", "seq", None),
            P("grp", "seq", None),
            P("grp", "seq", None),
            P(),
            P(),
            P(),
            P(),
        ),
        check_vma=False,
    )
```

profile of v0, /device:TPU:0, one launch (start us, length us, event | category | flops | bytes accessed | tf_op | source)
XLA Modules:
  0.0 1731.6 jit_solution(6610942294189539147)
XLA Ops:
  8.7 116.0 %all-gather.11.cloned.1.call-done = bf16[168,512,128]{2,1,0:T(8,128)(2,1)} async-done(((bf16[21,512,128]{2,1,0:T(8,128)(2,1)}), bf16[168,512,128]{2,1,0:T(8,128)(2,1)}) %all-gather.11.cloned.1.call-update) | async-done | bytes 22020112 | tf_op jit(solution)/shard_map/all_gather | solution.py:172
  134.4 48.4 %all-gather.13.cloned.1.call-done = bf16[4,64,4352]{2,1,0:T(8,128)(2,1)} async-done(((bf16[1,64,4352]{2,1,0:T(8,128)(2,1)}), bf16[4,64,4352]{2,1,0:T(8,128)(2,1)}) %all-gather.13.cloned.1.call-update) | async-done | bytes 2228240 | tf_op jit(solution)/shard_map/all_gather | solution.py:183
  204.3 73.6 %all-gather.15.cloned.1.call-done = bf16[4,512,4352]{2,1,0:T(8,128)(2,1)} async-done(((bf16[4,64,4352]{2,1,0:T(8,128)(2,1)}), bf16[4,512,4352]{2,1,0:T(8,128)(2,1)}) %all-gather.15.cloned.1.call-update) | async-done | bytes 17825808 | tf_op jit(solution)/shard_map/all_gather | solution.py:184
  296.3 40.8 %all-gather = s32[4,1,256]{2,1,0:T(1,128)S(1)} all-gather(s32[1,1,256]{2,1,0:T(1,128)} %bitcast.336), channel_id=1, replica_groups=mesh['grp'=8,'seq'=4] {'seq'}, dimensions={0}, use_global_device_ids=true | all-gather | bytes 5120 | tf_op jit(solution)/shard_map/all_gather | solution.py:213
  339.6 43.2 %all_gather.37 = bf16[1024,256]{0,1:T(8,128)(2,1)S(1)} all-gather(bf16[256,256]{0,1:T(8,128)(2,1)S(1)} %pad_maximum_fusion.11), channel_id=1, replica_groups=mesh['grp'=8,'seq'=4] {'seq'}, dimensions={0}, use_global_device_ids=true | all-gather | bytes 655360 | tf_op jit(solution)/shard_map/all_gather | solution.py:208
  388.0 17.3 while.36
  410.6 59.3 %all_to_all.61 = bf16[4,256,512]{2,1,0:T(8,128)(2,1)} all-to-all(bf16[4,256,512]{2,1,0:T(8,128)(2,1)} %convert_element_type.137), channel_id=1, replica_groups=mesh['grp'=8,'seq'=4] {'seq'}, dimensions={0} | all-to-all | bytes 2097152 | tf_op jit(solution)/shard_map/all_to_all | solution.py:223
  481.9 18.0 %all-gather.19.cloned.1.call-done = bf16[2048,2304]{0,1:T(8,128)(2,1)} async-done(((bf16[512,2304]{0,1:T(8,128)(2,1)}), bf16[2048,2304]{0,1:T(8,128)(2,1)}) %all-gather.19.cloned.1.call-update) | async-done | bytes 9437200 | tf_op jit(solution)/shard_map/all_gather | solution.py:191
  499.8 54.9 %all-gather.17.cloned.1.call-done = bf16[2048,2048]{1,0:T(8,128)(2,1)} async-done(((bf16[256,2048]{1,0:T(8,128)(2,1)}), bf16[2048,2048]{1,0:T(8,128)(2,1)}) %all-gather.17.cloned.1.call-update) | async-done | bytes 8388624 | tf_op jit(solution)/shard_map/all_gather | solution.py:234
  554.8 19.0 %fusion.95 = f32[2048,1536]{0,1:T(8,128)} fusion(bf16[2048,2048]{1,0:T(8,128)(2,1)} %all-gather.17.cloned.1.call-done, bf16[2048,2304]{0,1:T(8,128)(2,1)} %all-gather.19.cloned.1.call-done), kind=kOutput, calls=%fused_computation.134 | convolution fusion | flops 12884901888 | bytes 27262976 | tf_op jit(solution)/shard_map/dot_general | solution.py:237
  573.7 37.2 %all-gather.21.cloned.1.call-done = bf16[2048,2048]{1,0:T(8,128)(2,1)} async-done(((bf16[256,2048]{1,0:T(8,128)(2,1)}), bf16[2048,2048]{1,0:T(8,128)(2,1)}) %all-gather.21.cloned.1.call-update) | async-done | bytes 8388624 | tf_op jit(solution)/shard_map/all_gather | solution.py:192
  610.9 16.7 fusion.91
  629.3 18.7 %convolution_convert_fusion.3 = bf16[2048,2048]{1,0:T(8,128)(2,1)} fusion(bf16[2048,2304]{0,1:T(8,128)(2,1)} %all-gather.19.cloned.1.call-done, bf16[2048,768]{0,1:T(8,128)(2,1)} %get-tuple-element.680, bf16[2048,768]{0,1:T(8,128)(2,1)S(1)} %get-tuple-element.679), kind=kOutput, calls=%fused_computation.117 | convolution fusion | flops 12901679104 | bytes 20971520 | tf_op jit(solution)/shard_map/dot_general | solution.py:51
  648.1 11.9 convolution_convert_fusion.4
  660.0 59.5 %reduce-scatter.9.cloned.1.call-done = bf16[256,2048]{1,0:T(8,128)(2,1)} async-done(((bf16[2048,2048]{1,0:T(8,128)(2,1)}), bf16[256,2048]{1,0:T(8,128)(2,1)}) %reduce-scatter.9.cloned.1.call-update) | async-done | bytes 1048592 | tf_op jit(solution)/shard_map/reduce_scatter | solution.py:249
  722.5 72.2 %reduce-scatter.7.cloned.1.call-done = bf16[256,2048]{1,0:T(8,128)(2,1)} async-done(((bf16[2048,2048]{1,0:T(8,128)(2,1)}), bf16[256,2048]{1,0:T(8,128)(2,1)}) %reduce-scatter.7.cloned.1.call-update) | async-done | bytes 1048592 | tf_op jit(solution)/shard_map/reduce_scatter | solution.py:261
  811.1 25.8 %all-to-all-done.2 = bf16[256,4,512]{2,0,1:T(8,128)(2,1)} async-done(((bf16[256,4,512]{2,0,1:T(8,128)(2,1)}), bf16[256,4,512]{2,0,1:T(8,128)(2,1)}, u32[]{:S(2)}, u32[]{:S(2)}) %all-to-all-start.2) | async-done | bytes 1048608 | tf_op jit(solution)/shard_map/all_to_all | solution.py:279
  839.5 123.5 %while.37 = (s32[]{:T(128)}, f32[1024,128]{1,0:T(8,128)}, f32[1024,128]{1,0:T(8,128)}, f32[2,512,4,128]{3,1,0,2:T(8,128)}, s32[2,512]{1,0:T(2,128)S(1)}, /*index...) while((s32[]{:T(128)}, f32[1024,128]{1,0:T(8,128)}, ...), condition=%wide.region_11.12_spmd.clone.clone, body=%wide.region_9.11_spmd.clone.clone.sunk | while | flops 2742048256 | bytes 106783928 | solution.py:128
  850.3 22.8 %fusion.228 = f32[2,512,4,128]{3,1,0,2:T(8,128)} fusion(f32[2,512,4,128]{3,1,0,2:T(8,128)} %get-tuple-element.900, s32[]{:T(128)} %get-tuple-element.897, f32[512,4,1024]{2,0,1:T(8,128)} %fusion.223, f32[512,4,1024]{2,0,1:T(8,128)} %fusion.224, f32[4,512]{1,0:T(4,128)S(1)} %dynamic-slice_bitcast_fusion.2, pred[512,1024]{1,0:T(8,128)(4,1)} %fusion.225, ...), kind=kOutput, calls=%fused_computation.67.clone.1 | convolution fusion | flops 559942656 | bytes 35930624 | tf_op jit(solution)/shard_map/while/body/eval_jaxpr/hqk,kd->qhd/dot_general | solution.py:113
  873.1 21.3 %fusion.226 = f32[1024,128]{1,0:T(8,128)} fusion(f32[512,4,1024]{2,0,1:T(8,128)} %fusion.223, f32[512,4,1024]{2,0,1:T(8,128)} %fusion.224, f32[4,512]{1,0:T(4,128)S(1)} %dynamic-slice_bitcast_fusion.2, pred[512,1024]{1,0:T(8,128)(4,1)} %fusion.225, f32[1024,128]{1,0:T(8,128)} %get-tuple-element.898, ...), kind=kOutput, calls=%fused_computation.70.clone.1 | convolution fusion | flops 560204800 | bytes 36192768 | tf_op jit(solution)/shard_map/while/body/eval_jaxpr/hqk,qhd->kd/dot_general | solution.py:116
  912.0 22.8 %fusion.228 = f32[2,512,4,128]{3,1,0,2:T(8,128)} fusion(f32[2,512,4,128]{3,1,0,2:T(8,128)} %get-tuple-element.900, s32[]{:T(128)} %get-tuple-element.897, f32[512,4,1024]{2,0,1:T(8,128)} %fusion.223, f32[512,4,1024]{2,0,1:T(8,128)} %fusion.224, f32[4,512]{1,0:T(4,128)S(1)} %dynamic-slice_bitcast_fusion.2, pred[512,1024]{1,0:T(8,128)(4,1)} %fusion.225, ...), kind=kOutput, calls=%fused_computation.67.clone.1 | convolution fusion | flops 559942656 | bytes 35930624 | tf_op jit(solution)/shard_map/while/body/eval_jaxpr/hqk,kd->qhd/dot_general | solution.py:113
  934.8 21.3 %fusion.226 = f32[1024,128]{1,0:T(8,128)} fusion(f32[512,4,1024]{2,0,1:T(8,128)} %fusion.223, f32[512,4,1024]{2,0,1:T(8,128)} %fusion.224, f32[4,512]{1,0:T(4,128)S(1)} %dynamic-slice_bitcast_fusion.2, pred[512,1024]{1,0:T(8,128)(4,1)} %fusion.225, f32[1024,128]{1,0:T(8,128)} %get-tuple-element.898, ...), kind=kOutput, calls=%fused_computation.70.clone.1 | convolution fusion | flops 560204800 | bytes 36192768 | tf_op jit(solution)/shard_map/while/body/eval_jaxpr/hqk,qhd->kd/dot_general | solution.py:116
  977.2 41.2 %all_to_all.62 = bf16[4,256,512]{2,1,0:T(8,128)(2,1)} all-to-all(bf16[4,256,512]{2,1,0:T(8,128)(2,1)} %convert_element_type.151), channel_id=1, replica_groups=mesh['grp'=8,'seq'=4] {'seq'}, dimensions={0} | all-to-all | bytes 2097152 | tf_op jit(solution)/shard_map/all_to_all | solution.py:306
  1062.7 15.9 convolution_convert_fusion.1
  1078.6 11.5 pad_maximum_fusion
  1090.2 79.3 %reduce-scatter.13.cloned.1.call-done = bf16[64,2304]{1,0:T(8,128)(2,1)} async-done(((bf16[2048,2304]{1,0:T(8,128)(2,1)}), bf16[64,2304]{1,0:T(8,128)(2,1)}) %reduce-scatter.13.cloned.1.call-update) | async-done | bytes 294928 | tf_op jit(solution)/shard_map/reduce_scatter | solution.py:288
  1169.6 187.0 %reduce-scatter.15.cloned.1.call-done = bf16[64,2048]{1,0:T(8,128)(2,1)} async-done(((bf16[2048,2048]{1,0:T(8,128)(2,1)}), bf16[64,2048]{1,0:T(8,128)(2,1)}) %reduce-scatter.15.cloned.1.call-update) | async-done | bytes 262160 | tf_op jit(solution)/shard_map/reduce_scatter | solution.py:288
  1356.7 161.1 %reduce-scatter.17.cloned.1.call-done = bf16[512,2304]{0,1:T(8,128)(2,1)} async-done(((bf16[2048,2304]{0,1:T(8,128)(2,1)}), bf16[512,2304]{0,1:T(8,128)(2,1)}) %reduce-scatter.17.cloned.1.call-update) | async-done | bytes 2359312 | tf_op jit(solution)/shard_map/reduce_scatter | solution.py:258
  1534.5 41.6 %psum.7 = f32[2,2048]{1,0:T(2,128)S(1)} all-reduce(f32[2,2048]{1,0:T(2,128)S(1)} %pad_maximum_fusion.12), channel_id=1, replica_groups=mesh['grp'=8,'seq'=4] {'grp','seq'}, use_global_device_ids=true, to_apply=%region_20.21 | all-reduce | flops 4096 | bytes 32768 | tf_op jit(solution)/shard_map/psum | solution.py:322
  1605.0 76.1 %all-gather.27.cloned.1.call-done = bf16[144,512,128]{2,1,0:T(8,128)(2,1)} async-done(((bf16[18,512,128]{2,1,0:T(8,128)(2,1)}), bf16[144,512,128]{2,1,0:T(8,128)(2,1)}) %all-gather.27.cloned.1.call-update) | async-done | bytes 18874384 | tf_op jit(solution)/shard_map/all_gather | solution.py:260
  1690.0 18.5 %fusion.97 = (f32[21,512,128]{2,1,0:T(8,128)}, f32[21,512,128]{2,1,0:T(8,128)}) fusion(f32[21,512,128]{2,1,0:T(8,128)} %param.24, f32[21,512,128]{2,1,0:T(8,128)} %param.23, f32[21,128,128]{2,1,0:T(8,128)S(1)} %copy-done, f32[21,512,512]{2,1,0:T(8,128)} %param.25, bf16[21,512,128]{2,1,0:T(8,128)(2,1)} %gather_fusion.3, ...), kind=kOutput, calls=%fused_computation.136 | convolution fusion | flops 1772617728 | bytes 50921512 | tf_op jit(solution)/shard_map/zic,zcd->zid/dot_general | solution.py:344
  1708.5 16.1 multiply_subtract_fusion
  (235 shorter events, 264.9 us)
Async XLA Ops:
  7.2 1682.9 %copy-start = (f32[21,128,128]{2,1,0:T(8,128)S(1)}, f32[21,128,128]{2,1,0:T(8,128)}, u32[]{:S(2)}) copy-start(f32[21,128,128]{2,1,0:T(8,128)} %param.26) | copy-start | bytes 4128772
  7.2 117.5 %all-gather.11.cloned.1.call-start = ((), (), s32[]{:S(2)}) async-start(), calls=%async_computation.10 | async-start | bytes 24772608 | tf_op jit(solution)/shard_map/all_gather | solution.py:172
  7.9 174.9 %all-gather.13.cloned.1.call-start = ((), (), s32[]{:S(2)}) async-start(), calls=%async_computation.11 | async-start | bytes 2785280 | tf_op jit(solution)/shard_map/all_gather | solution.py:183
  8.7 174.4 %copy-start.1 = (s32[166]{0:T(256)S(1)}, s32[166]{0:T(256)}, u32[]{:S(2)}) copy-start(s32[166]{0:T(256)} %param.20) | copy-start | bytes 1996
  8.7 175.3 %copy-start.7 = (bf16[256,2048]{1,0:T(8,128)(2,1)S(1)}, bf16[256,2048]{1,0:T(8,128)(2,1)}, u32[]{:S(2)}) copy-start(bf16[256,2048]{1,0:T(8,128)(2,1)} %param.17) | copy-start | bytes 3145732
  134.4 143.5 %all-gather.15.cloned.1.call-start = ((), (), s32[]{:S(2)}) async-start(), calls=%async_computation.12 | async-start | bytes 20054016 | tf_op jit(solution)/shard_map/all_gather | solution.py:184
  182.9 317.0 %all-gather.19.cloned.1.call-start = ((), (), s32[]{:S(2)}) async-start(), calls=%async_computation.14 | async-start | bytes 11796480 | tf_op jit(solution)/shard_map/all_gather | solution.py:191
  202.7 136.5 %copy-start.22 = (f32[64]{0:T(128)}, f32[64]{0:T(128)S(1)}, u32[]{:S(2)}) copy-start(f32[64]{0:T(128)S(1)} %multiply_power_fusion) | copy-start | bytes 772
  203.3 80.9 %copy-start.19 = (f32[256]{0:T(256)}, f32[256]{0:T(256)S(1)}, u32[]{:S(2)}) copy-start(f32[256]{0:T(256)S(1)} %get-tuple-element.703) | copy-start | bytes 3076
  204.3 80.0 %copy-start.13 = (f32[1,2048]{1,0:T(1,128)}, f32[1,2048]{1,0:T(1,128)S(1)}, u32[]{:S(2)}) copy-start(f32[1,2048]{1,0:T(1,128)S(1)} %get-tuple-element.697) | copy-start | bytes 24580
  291.7 91.5 %all-to-all-start = ((bf16[256,4,512]{0,2,1:T(8,128)(2,1)}), bf16[256,4,512]{0,2,1:T(8,128)(2,1)S(1)}, u32[]{:S(2)}, u32[]{:S(2)}) async-start(bf16[256,4,512]{0,2,1:T(8,128)(2,1)} %bitcast.5), calls=%async_computation | async-start | bytes 2097152 | tf_op jit(solution)/shard_map/all_to_all | solution.py:217
  296.3 258.4 %all-gather.17.cloned.1.call-start = ((), (), s32[]{:S(2)}) async-start(), calls=%async_computation.13 | async-start | bytes 9437184 | tf_op jit(solution)/shard_map/all_gather | solution.py:234
  481.1 129.9 %all-gather.21.cloned.1.call-start = ((), (), s32[]{:S(2)}) async-start(), calls=%async_computation.16 | async-start | bytes 9437184 | tf_op jit(solution)/shard_map/all_gather | solution.py:192
  481.7 237.9 %reduce-scatter.9.cloned.1.call-start = ((), (), s32[]{:S(2)}) async-start(), calls=%async_computation.17 | async-start | bytes 9437184 | tf_op jit(solution)/shard_map/reduce_scatter | solution.py:249
  648.1 146.6 %reduce-scatter.7.cloned.1.call-start = ((), (), s32[]{:S(2)}) async-start(), calls=%async_computation.15 | async-start | bytes 9437184 | tf_op jit(solution)/shard_map/reduce_scatter | solution.py:261
  806.5 30.4 %all-to-all-start.2 = ((bf16[256,4,512]{2,0,1:T(8,128)(2,1)}), bf16[256,4,512]{2,0,1:T(8,128)(2,1)}, u32[]{:S(2)}, u32[]{:S(2)}) async-start(bf16[256,4,512]{2,0,1:T(8,128)(2,1)} %bitcast.312), calls=%async_computation.4 | async-start | bytes 2097152 | tf_op jit(solution)/shard_map/all_to_all | solution.py:279
  811.1 208.7 %reduce-scatter.11.cloned.1.call-start = ((), (), s32[]{:S(2)}) async-start(), calls=%async_computation.18 | async-start | bytes 1310720 | tf_op jit(solution)/shard_map/reduce_scatter | solution.py:308
  839.5 127.7 %copy-start.23 = (f32[64]{0:T(128)S(1)}, f32[64]{0:T(128)}, u32[]{:S(2)}) copy-start(f32[64]{0:T(128)} %copy-done.22) | copy-start | bytes 772
  971.8 197.8 %reduce-scatter.13.cloned.1.call-start = ((), (), s32[]{:S(2)}) async-start(), calls=%async_computation.19 | async-start | bytes 9732096 | tf_op jit(solution)/shard_map/reduce_scatter | solution.py:288
  974.5 46.6 %copy-start.8 = (bf16[256,2048]{1,0:T(8,128)(2,1)S(1)}, bf16[256,2048]{1,0:T(8,128)(2,1)}, u32[]{:S(2)}) copy-start(bf16[256,2048]{1,0:T(8,128)(2,1)} %param.17) | copy-start | bytes 3145732
  974.5 46.6 %copy-start.14 = (f32[1,2048]{1,0:T(1,128)S(1)}, f32[1,2048]{1,0:T(1,128)}, u32[]{:S(2)}) copy-start(f32[1,2048]{1,0:T(1,128)} %copy-done.13) | copy-start | bytes 24580
  974.5 46.6 %copy-start.20 = (f32[256]{0:T(256)S(1)}, f32[256]{0:T(256)}, u32[]{:S(2)}) copy-start(f32[256]{0:T(256)} %copy-done.19) | copy-start | bytes 3076
  1034.7 321.9 %reduce-scatter.15.cloned.1.call-start = ((), (), s32[]{:S(2)}) async-start(), calls=%async_computation.21 | async-start | bytes 8650752 | tf_op jit(solution)/shard_map/reduce_scatter | solution.py:288
  1051.9 465.9 %reduce-scatter.17.cloned.1.call-start = ((), (), s32[]{:S(2)}) async-start(), calls=%async_computation.23 | async-start | bytes 11796480 | tf_op jit(solution)/shard_map/reduce_scatter | solution.py:258
  1090.1 432.0 %copy-start.2 = (s32[166]{0:T(256)S(1)}, s32[166]{0:T(256)}, u32[]{:S(2)}) copy-start(s32[166]{0:T(256)} %param.20) | copy-start | bytes 1996
  1090.2 491.9 %all-gather.23.cloned.1.call-start = ((), (), s32[]{:S(2)}) async-start(), calls=%async_computation.20 | async-start | bytes 2654208 | tf_op jit(solution)/shard_map/all_gather | solution.py:289
  1169.5 412.5 %all-gather.25.cloned.1.call-start = ((), (), s32[]{:S(2)}) async-start(), calls=%async_computation.22 | async-start | bytes 2359296 | tf_op jit(solution)/shard_map/all_gather | solution.py:289
  1356.6 324.5 %all-gather.27.cloned.1.call-start = ((), (), s32[]{:S(2)}) async-start(), calls=%async_computation.24 | async-start | bytes 21233664 | tf_op jit(solution)/shard_map/all_gather | solution.py:260
  1525.1 51.6 %copy-start.16 = (f32[2,2048]{1,0:T(2,128)S(1)}, f32[2,2048]{1,0:T(2,128)}, u32[]{:S(2)}) copy-start(f32[2,2048]{1,0:T(2,128)} %param.27) | copy-start | bytes 49156
  1525.1 51.6 %copy-start.21 = (f32[2,2048]{1,0:T(2,128)S(1)}, f32[2,2048]{1,0:T(2,128)}, u32[]{:S(2)}) copy-start(f32[2,2048]{1,0:T(2,128)} %param.28) | copy-start | bytes 49156
  1600.1 90.0 %copy-start.24 = (pred[21]{0:T(512)(128)(4,1)S(1)}, pred[21]{0:T(512)(128)(4,1)}, u32[]{:S(2)}) copy-start(pred[21]{0:T(512)(128)(4,1)} %get-tuple-element.671) | copy-start | bytes 67
  1600.1 90.0 %copy-start.25 = (pred[21]{0:T(512)(128)(4,1)S(1)}, pred[21]{0:T(512)(128)(4,1)}, u32[]{:S(2)}) copy-start(pred[21]{0:T(512)(128)(4,1)} %broadcast_compare_fusion) | copy-start | bytes 67
  (15 other events, 98.3 us)
Sparse Core Ops, SparseCore 0:
  9.9 114.7 all-gather.10
  134.5 48.3 all-gather.12
  184.8 93.1 all-gather.14
  279.9 219.8 all-gather.18
  502.1 52.5 all-gather.16
  556.5 54.3 all-gather.20
  648.2 71.2 reduce-scatter.8
  723.4 71.2 reduce-scatter.6
  971.9 35.7 reduce-scatter.10
  1034.8 134.6 reduce-scatter.12
  1171.8 184.7 reduce-scatter.14
  1358.8 158.9 reduce-scatter.16
  1519.7 30.3 all-gather.22
  1551.9 28.3 all-gather.24
  1582.5 98.5 all-gather.26
where the time goes:
time: 1740 us; the launch traced here: 1730 us
  waiting for transfers between devices  1010 us (58%)
  matrix products  299 us (17%)
  blocking collectives  226 us (13%)
  local copies, waits for them, and re-layouts  112 us (6%)
  other arithmetic  59.6 us (3%)
    reduce_scatter x2, waiting for transfers between devices, reduce_rows(): lax.psum_scatter(blocks, ('grp', 'seq'), scatter_dimension=0, tiled=True)  266 us
    reduce_scatter x1, waiting for transfers between devices, local(): lax.psum_scatter(feed_grads, 'seq', scatter_dimension=0, tiled=True)  161 us
    all_gather x1, waiting for transfers between devices, local(): plane_tiles = lax.all_gather(weights_low, 'grp', axis=0, tiled=True)  116 us
    all_gather x1, waiting for transfers between devices, local(): feed_grads = lax.all_gather(feed_grads, 'grp', axis=0, tiled=True)  76.1 us
    all_gather x1, waiting for transfers between devices, local(): lax.all_gather(attn_weights, 'grp', axis=1, tiled=True)  73.6 us
    reduce_scatter x1, waiting for transfers between devices, local(): lax.psum_scatter(times_transpose(activated, down_weights).astype(jnp.bflo...  72.2 us
    reduce_scatter x1, waiting for transfers between devices, local(): lax.psum_scatter(times_transpose(gating_grad, gating_weights).astype(jnp....  59.5 us
    all_to_all x1, blocking collectives, local(): lax.all_to_all(head_context.reshape(-1, heads_here * HD).astype(jnp.bfloa...  59.3 us
  transfers between devices with their start and end apart: 17, of which 13 were waited for; matrix products, arithmetic and copies ran while one was open for 12% of the time, Pallas kernels for 0%

commit v1 on v0

--- a/solution.py
+++ b/solution.py
@@ -319,7 +319,8 @@
         * inverse_one**3
         * jnp.mean(tok_float * gains[0] * norm_one_grad, axis=-1, keepdims=True)
     )
-    gain_grads = lax.psum(jnp.stack([gain_one_term, gain_two_term]), ("grp", "seq"))
+    xs = jnp.stack([gain_one_term, gain_two_term])
+    gain_grads = jax.lax.all_gather(xs, axis_name=("grp", "seq")).sum(axis=0)
     tile_count = tile_owner_slots.shape[0]
     tile_of_slot = (
         jnp.full((grp_count * slots_here,), tile_count, jnp.int32)

time: 1740 us -> 1740 us (level)
  blocking collectives: 226 us -> 263 us
  waiting for transfers between devices: 1010 us -> 974 us
    all_gather x0 -> x1, blocking collectives: none -> 78 us  [local(): gain_grads = jax.lax.all_gather(xs, axis_name=('grp', 'seq')).sum(axis=0)]
    psum x1 -> x0, blocking collectives: 41.6 us -> none  [local(): lax.psum(jnp.stack([gain_one_term, gain_two_term]), ('grp', 'seq'))]
    all_gather x1, waiting for transfers between devices: 76.1 us -> 39.9 us  [local(): feed_grads = lax.all_gather(feed_grads, 'grp', axis=0, tiled=True)]
where the time goes in v1:
time: 1740 us; the launch traced here: 1730 us
  waiting for transfers between devices  974 us (56%)
  matrix products  299 us (17%)
  blocking collectives  263 us (15%)
  local copies, waits for them, and re-layouts  111 us (6%)
  other arithmetic  60 us (3%)
    reduce_scatter x2, waiting for transfers between devices, reduce_rows(): lax.psum_scatter(blocks, ('grp', 'seq'), scatter_dimension=0, tiled=True)  266 us
    reduce_scatter x1, waiting for transfers between devices, local(): lax.psum_scatter(feed_grads, 'seq', scatter_dimension=0, tiled=True)  161 us
    all_gather x1, waiting for transfers between devices, local(): plane_tiles = lax.all_gather(weights_low, 'grp', axis=0, tiled=True)  116 us
    all_gather x1, blocking collectives, local(): gain_grads = jax.lax.all_gather(xs, axis_name=('grp', 'seq')).sum(axis=0)  78 us
    all_gather x1, waiting for transfers between devices, local(): lax.all_gather(attn_weights, 'grp', axis=1, tiled=True)  73.6 us
    reduce_scatter x1, waiting for transfers between devices, local(): lax.psum_scatter(times_transpose(activated, down_weights).astype(jnp.bflo...  72.2 us
    reduce_scatter x1, waiting for transfers between devices, local(): lax.psum_scatter(times_transpose(gating_grad, gating_weights).astype(jnp....  59.5 us
    all_to_all x1, blocking collectives, local(): lax.all_to_all(head_context.reshape(-1, heads_here * HD).astype(jnp.bfloa...  59.3 us
  transfers between devices with their start and end apart: 17, of which 13 were waited for; matrix products, arithmetic and copies ran while one was open for 12% of the time, Pallas kernels for 0%

profile of v1, /device:TPU:0, one launch (start us, length us, event | category | flops | bytes accessed | tf_op | source)
XLA Modules:
  0.0 1732.1 jit_solution(3158003115021907554)
XLA Ops:
  8.7 116.0 %all-gather.13.cloned.1.call-done = bf16[168,512,128]{2,1,0:T(8,128)(2,1)} async-done(((bf16[21,512,128]{2,1,0:T(8,128)(2,1)}), bf16[168,512,128]{2,1,0:T(8,128)(2,1)}) %all-gather.13.cloned.1.call-update) | async-done | bytes 22020112 | tf_op jit(solution)/shard_map/all_gather | solution.py:172
  134.4 48.4 %all-gather.15.cloned.1.call-done = bf16[4,64,4352]{2,1,0:T(8,128)(2,1)} async-done(((bf16[1,64,4352]{2,1,0:T(8,128)(2,1)}), bf16[4,64,4352]{2,1,0:T(8,128)(2,1)}) %all-gather.15.cloned.1.call-update) | async-done | bytes 2228240 | tf_op jit(solution)/shard_map/all_gather | solution.py:183
  204.3 73.6 %all-gather.17.cloned.1.call-done = bf16[4,512,4352]{2,1,0:T(8,128)(2,1)} async-done(((bf16[4,64,4352]{2,1,0:T(8,128)(2,1)}), bf16[4,512,4352]{2,1,0:T(8,128)(2,1)}) %all-gather.17.cloned.1.call-update) | async-done | bytes 17825808 | tf_op jit(solution)/shard_map/all_gather | solution.py:184
  296.3 40.8 %all-gather.1 = s32[4,1,256]{2,1,0:T(1,128)S(1)} all-gather(s32[1,1,256]{2,1,0:T(1,128)} %bitcast.338), channel_id=1, replica_groups=mesh['grp'=8,'seq'=4] {'seq'}, dimensions={0}, use_global_device_ids=true | all-gather | bytes 5120 | tf_op jit(solution)/shard_map/all_gather | solution.py:213
  339.6 43.2 %all_gather.43 = bf16[1024,256]{0,1:T(8,128)(2,1)S(1)} all-gather(bf16[256,256]{0,1:T(8,128)(2,1)S(1)} %pad_maximum_fusion.11), channel_id=1, replica_groups=mesh['grp'=8,'seq'=4] {'seq'}, dimensions={0}, use_global_device_ids=true | all-gather | bytes 655360 | tf_op jit(solution)/shard_map/all_gather | solution.py:208
  388.0 17.3 while.36
  410.6 59.3 %all_to_all.61 = bf16[4,256,512]{2,1,0:T(8,128)(2,1)} all-to-all(bf16[4,256,512]{2,1,0:T(8,128)(2,1)} %convert_element_type.137), channel_id=1, replica_groups=mesh['grp'=8,'seq'=4] {'seq'}, dimensions={0} | all-to-all | bytes 2097152 | tf_op jit(solution)/shard_map/all_to_all | solution.py:223
  481.9 17.9 %all-gather.21.cloned.1.call-done = bf16[2048,2304]{0,1:T(8,128)(2,1)} async-done(((bf16[512,2304]{0,1:T(8,128)(2,1)}), bf16[2048,2304]{0,1:T(8,128)(2,1)}) %all-gather.21.cloned.1.call-update) | async-done | bytes 9437200 | tf_op jit(solution)/shard_map/all_gather | solution.py:191
  499.8 54.9 %all-gather.19.cloned.1.call-done = bf16[2048,2048]{1,0:T(8,128)(2,1)} async-done(((bf16[256,2048]{1,0:T(8,128)(2,1)}), bf16[2048,2048]{1,0:T(8,128)(2,1)}) %all-gather.19.cloned.1.call-update) | async-done | bytes 8388624 | tf_op jit(solution)/shard_map/all_gather | solution.py:234
  554.8 19.1 %fusion.95 = f32[2048,1536]{0,1:T(8,128)} fusion(bf16[2048,2048]{1,0:T(8,128)(2,1)} %all-gather.19.cloned.1.call-done, bf16[2048,2304]{0,1:T(8,128)(2,1)} %all-gather.21.cloned.1.call-done), kind=kOutput, calls=%fused_computation.134 | convolution fusion | flops 12884901888 | bytes 27262976 | tf_op jit(solution)/shard_map/dot_general | solution.py:237
  573.9 37.1 %all-gather.23.cloned.1.call-done = bf16[2048,2048]{1,0:T(8,128)(2,1)} async-done(((bf16[256,2048]{1,0:T(8,128)(2,1)}), bf16[2048,2048]{1,0:T(8,128)(2,1)}) %all-gather.23.cloned.1.call-update) | async-done | bytes 8388624 | tf_op jit(solution)/shard_map/all_gather | solution.py:192
  610.9 16.7 fusion.91
  629.3 18.7 %convolution_convert_fusion.3 = bf16[2048,2048]{1,0:T(8,128)(2,1)} fusion(bf16[2048,2304]{0,1:T(8,128)(2,1)} %all-gather.21.cloned.1.call-done, bf16[2048,768]{0,1:T(8,128)(2,1)} %get-tuple-element.680, bf16[2048,768]{0,1:T(8,128)(2,1)S(1)} %get-tuple-element.679), kind=kOutput, calls=%fused_computation.117 | convolution fusion | flops 12901679104 | bytes 20971520 | tf_op jit(solution)/shard_map/dot_general | solution.py:51
  648.1 11.9 convolution_convert_fusion.4
  660.0 59.5 %reduce-scatter.9.cloned.1.call-done = bf16[256,2048]{1,0:T(8,128)(2,1)} async-done(((bf16[2048,2048]{1,0:T(8,128)(2,1)}), bf16[256,2048]{1,0:T(8,128)(2,1)}) %reduce-scatter.9.cloned.1.call-update) | async-done | bytes 1048592 | tf_op jit(solution)/shard_map/reduce_scatter | solution.py:249
  722.5 72.2 %reduce-scatter.7.cloned.1.call-done = bf16[256,2048]{1,0:T(8,128)(2,1)} async-done(((bf16[2048,2048]{1,0:T(8,128)(2,1)}), bf16[256,2048]{1,0:T(8,128)(2,1)}) %reduce-scatter.7.cloned.1.call-update) | async-done | bytes 1048592 | tf_op jit(solution)/shard_map/reduce_scatter | solution.py:261
  811.1 25.8 %all-to-all-done.2 = bf16[256,4,512]{2,0,1:T(8,128)(2,1)} async-done(((bf16[256,4,512]{2,0,1:T(8,128)(2,1)}), bf16[256,4,512]{2,0,1:T(8,128)(2,1)}, u32[]{:S(2)}, u32[]{:S(2)}) %all-to-all-start.2) | async-done | bytes 1048608 | tf_op jit(solution)/shard_map/all_to_all | solution.py:279
  839.5 123.4 %while.37 = (s32[]{:T(128)}, f32[1024,128]{1,0:T(8,128)}, f32[1024,128]{1,0:T(8,128)}, f32[2,512,4,128]{3,1,0,2:T(8,128)}, s32[2,512]{1,0:T(2,128)S(1)}, /*index...) while((s32[]{:T(128)}, f32[1024,128]{1,0:T(8,128)}, ...), condition=%wide.region_11.12_spmd.clone.clone, body=%wide.region_9.11_spmd.clone.clone.sunk | while | flops 2742048256 | bytes 106783928 | solution.py:128
  850.3 22.8 %fusion.228 = f32[2,512,4,128]{3,1,0,2:T(8,128)} fusion(f32[2,512,4,128]{3,1,0,2:T(8,128)} %get-tuple-element.900, s32[]{:T(128)} %get-tuple-element.897, f32[512,4,1024]{2,0,1:T(8,128)} %fusion.223, f32[512,4,1024]{2,0,1:T(8,128)} %fusion.224, f32[4,512]{1,0:T(4,128)S(1)} %dynamic-slice_bitcast_fusion.2, pred[512,1024]{1,0:T(8,128)(4,1)} %fusion.225, ...), kind=kOutput, calls=%fused_computation.67.clone.1 | convolution fusion | flops 559942656 | bytes 35930624 | tf_op jit(solution)/shard_map/while/body/eval_jaxpr/hqk,kd->qhd/dot_general | solution.py:113
  873.2 21.2 %fusion.226 = f32[1024,128]{1,0:T(8,128)} fusion(f32[512,4,1024]{2,0,1:T(8,128)} %fusion.223, f32[512,4,1024]{2,0,1:T(8,128)} %fusion.224, f32[4,512]{1,0:T(4,128)S(1)} %dynamic-slice_bitcast_fusion.2, pred[512,1024]{1,0:T(8,128)(4,1)} %fusion.225, f32[1024,128]{1,0:T(8,128)} %get-tuple-element.898, ...), kind=kOutput, calls=%fused_computation.70.clone.1 | convolution fusion | flops 560204800 | bytes 36192768 | tf_op jit(solution)/shard_map/while/body/eval_jaxpr/hqk,qhd->kd/dot_general | solution.py:116
  911.9 22.9 %fusion.228 = f32[2,512,4,128]{3,1,0,2:T(8,128)} fusion(f32[2,512,4,128]{3,1,0,2:T(8,128)} %get-tuple-element.900, s32[]{:T(128)} %get-tuple-element.897, f32[512,4,1024]{2,0,1:T(8,128)} %fusion.223, f32[512,4,1024]{2,0,1:T(8,128)} %fusion.224, f32[4,512]{1,0:T(4,128)S(1)} %dynamic-slice_bitcast_fusion.2, pred[512,1024]{1,0:T(8,128)(4,1)} %fusion.225, ...), kind=kOutput, calls=%fused_computation.67.clone.1 | convolution fusion | flops 559942656 | bytes 35930624 | tf_op jit(solution)/shard_map/while/body/eval_jaxpr/hqk,kd->qhd/dot_general | solution.py:113
  934.7 21.3 %fusion.226 = f32[1024,128]{1,0:T(8,128)} fusion(f32[512,4,1024]{2,0,1:T(8,128)} %fusion.223, f32[512,4,1024]{2,0,1:T(8,128)} %fusion.224, f32[4,512]{1,0:T(4,128)S(1)} %dynamic-slice_bitcast_fusion.2, pred[512,1024]{1,0:T(8,128)(4,1)} %fusion.225, f32[1024,128]{1,0:T(8,128)} %get-tuple-element.898, ...), kind=kOutput, calls=%fused_computation.70.clone.1 | convolution fusion | flops 560204800 | bytes 36192768 | tf_op jit(solution)/shard_map/while/body/eval_jaxpr/hqk,qhd->kd/dot_general | solution.py:116
  977.1 41.2 %all_to_all.62 = bf16[4,256,512]{2,1,0:T(8,128)(2,1)} all-to-all(bf16[4,256,512]{2,1,0:T(8,128)(2,1)} %convert_element_type.151), channel_id=1, replica_groups=mesh['grp'=8,'seq'=4] {'seq'}, dimensions={0} | all-to-all | bytes 2097152 | tf_op jit(solution)/shard_map/all_to_all | solution.py:306
  1062.7 15.9 convolution_convert_fusion.1
  1078.6 11.5 pad_maximum_fusion
  1090.2 79.0 %reduce-scatter.13.cloned.1.call-done = bf16[64,2304]{1,0:T(8,128)(2,1)} async-done(((bf16[2048,2304]{1,0:T(8,128)(2,1)}), bf16[64,2304]{1,0:T(8,128)(2,1)}) %reduce-scatter.13.cloned.1.call-update) | async-done | bytes 294928 | tf_op jit(solution)/shard_map/reduce_scatter | solution.py:288
  1169.3 187.3 %reduce-scatter.15.cloned.1.call-done = bf16[64,2048]{1,0:T(8,128)(2,1)} async-done(((bf16[2048,2048]{1,0:T(8,128)(2,1)}), bf16[64,2048]{1,0:T(8,128)(2,1)}) %reduce-scatter.15.cloned.1.call-update) | async-done | bytes 262160 | tf_op jit(solution)/shard_map/reduce_scatter | solution.py:288
  1356.6 161.1 %reduce-scatter.17.cloned.1.call-done = bf16[512,2304]{0,1:T(8,128)(2,1)} async-done(((bf16[2048,2304]{0,1:T(8,128)(2,1)}), bf16[512,2304]{0,1:T(8,128)(2,1)}) %reduce-scatter.17.cloned.1.call-update) | async-done | bytes 2359312 | tf_op jit(solution)/shard_map/reduce_scatter | solution.py:258
  1534.4 78.0 %all-gather.2 = f32[32,2,2048]{2,1,0:T(2,128)} all-gather(f32[1,2,2048]{2,1,0:T(2,128)S(1)} %maximum_bitcast_fusion.2), channel_id=2, replica_groups=mesh['grp'=8,'seq'=4] {'grp','seq'}, dimensions={0}, use_global_device_ids=true | all-gather | bytes 540672 | tf_op jit(solution)/shard_map/all_gather | solution.py:323
  1641.7 39.9 %all-gather.29.cloned.1.call-done = bf16[144,512,128]{2,1,0:T(8,128)(2,1)} async-done(((bf16[18,512,128]{2,1,0:T(8,128)(2,1)}), bf16[144,512,128]{2,1,0:T(8,128)(2,1)}) %all-gather.29.cloned.1.call-update) | async-done | bytes 18874384 | tf_op jit(solution)/shard_map/all_gather | solution.py:260
  1690.5 18.5 %fusion.97 = (f32[21,512,128]{2,1,0:T(8,128)}, f32[21,512,128]{2,1,0:T(8,128)}) fusion(f32[21,512,128]{2,1,0:T(8,128)} %param.24, f32[21,512,128]{2,1,0:T(8,128)} %param.23, f32[21,128,128]{2,1,0:T(8,128)S(1)} %copy-done, f32[21,512,512]{2,1,0:T(8,128)} %param.25, bf16[21,512,128]{2,1,0:T(8,128)(2,1)} %gather_fusion.3, ...), kind=kOutput, calls=%fused_computation.136 | convolution fusion | flops 1772617728 | bytes 50921512 | tf_op jit(solution)/shard_map/zic,zcd->zid/dot_general | solution.py:345
  1709.0 16.1 multiply_subtract_fusion
  (238 shorter events, 265.4 us)
Async XLA Ops:
  7.2 1683.3 %copy-start = (f32[21,128,128]{2,1,0:T(8,128)S(1)}, f32[21,128,128]{2,1,0:T(8,128)}, u32[]{:S(2)}) copy-start(f32[21,128,128]{2,1,0:T(8,128)} %param.26) | copy-start | bytes 4128772
  7.2 117.5 %all-gather.13.cloned.1.call-start = ((), (), s32[]{:S(2)}) async-start(), calls=%async_computation.10 | async-start | bytes 24772608 | tf_op jit(solution)/shard_map/all_gather | solution.py:172
  7.9 174.9 %all-gather.15.cloned.1.call-start = ((), (), s32[]{:S(2)}) async-start(), calls=%async_computation.11 | async-start | bytes 2785280 | tf_op jit(solution)/shard_map/all_gather | solution.py:183
  8.7 174.4 %copy-start.1 = (s32[166]{0:T(256)S(1)}, s32[166]{0:T(256)}, u32[]{:S(2)}) copy-start(s32[166]{0:T(256)} %param.20) | copy-start | bytes 1996
  8.7 175.3 %copy-start.7 = (bf16[256,2048]{1,0:T(8,128)(2,1)S(1)}, bf16[256,2048]{1,0:T(8,128)(2,1)}, u32[]{:S(2)}) copy-start(bf16[256,2048]{1,0:T(8,128)(2,1)} %param.17) | copy-start | bytes 3145732
  134.4 143.5 %all-gather.17.cloned.1.call-start = ((), (), s32[]{:S(2)}) async-start(), calls=%async_computation.12 | async-start | bytes 20054016 | tf_op jit(solution)/shard_map/all_gather | solution.py:184
  182.9 317.0 %all-gather.21.cloned.1.call-start = ((), (), s32[]{:S(2)}) async-start(), calls=%async_computation.14 | async-start | bytes 11796480 | tf_op jit(solution)/shard_map/all_gather | solution.py:191
  202.7 136.5 %copy-start.23 = (f32[64]{0:T(128)}, f32[64]{0:T(128)S(1)}, u32[]{:S(2)}) copy-start(f32[64]{0:T(128)S(1)} %multiply_power_fusion) | copy-start | bytes 772
  203.3 81.0 %copy-start.19 = (f32[256]{0:T(256)}, f32[256]{0:T(256)S(1)}, u32[]{:S(2)}) copy-start(f32[256]{0:T(256)S(1)} %get-tuple-element.703) | copy-start | bytes 3076
  204.3 80.0 %copy-start.13 = (f32[1,2048]{1,0:T(1,128)}, f32[1,2048]{1,0:T(1,128)S(1)}, u32[]{:S(2)}) copy-start(f32[1,2048]{1,0:T(1,128)S(1)} %get-tuple-element.697) | copy-start | bytes 24580
  291.7 91.5 %all-to-all-start = ((bf16[256,4,512]{0,2,1:T(8,128)(2,1)}), bf16[256,4,512]{0,2,1:T(8,128)(2,1)S(1)}, u32[]{:S(2)}, u32[]{:S(2)}) async-start(bf16[256,4,512]{0,2,1:T(8,128)(2,1)} %bitcast.5), calls=%async_computation | async-start | bytes 2097152 | tf_op jit(solution)/shard_map/all_to_all | solution.py:217
  296.3 258.4 %all-gather.19.cloned.1.call-start = ((), (), s32[]{:S(2)}) async-start(), calls=%async_computation.13 | async-start | bytes 9437184 | tf_op jit(solution)/shard_map/all_gather | solution.py:234
  481.1 129.8 %all-gather.23.cloned.1.call-start = ((), (), s32[]{:S(2)}) async-start(), calls=%async_computation.16 | async-start | bytes 9437184 | tf_op jit(solution)/shard_map/all_gather | solution.py:192
  481.7 237.7 %reduce-scatter.9.cloned.1.call-start = ((), (), s32[]{:S(2)}) async-start(), calls=%async_computation.17 | async-start | bytes 9437184 | tf_op jit(solution)/shard_map/reduce_scatter | solution.py:249
  648.0 146.6 %reduce-scatter.7.cloned.1.call-start = ((), (), s32[]{:S(2)}) async-start(), calls=%async_computation.15 | async-start | bytes 9437184 | tf_op jit(solution)/shard_map/reduce_scatter | solution.py:261
  806.5 30.4 %all-to-all-start.2 = ((bf16[256,4,512]{2,0,1:T(8,128)(2,1)}), bf16[256,4,512]{2,0,1:T(8,128)(2,1)}, u32[]{:S(2)}, u32[]{:S(2)}) async-start(bf16[256,4,512]{2,0,1:T(8,128)(2,1)} %bitcast.314), calls=%async_computation.4 | async-start | bytes 2097152 | tf_op jit(solution)/shard_map/all_to_all | solution.py:279
  811.1 208.7 %reduce-scatter.11.cloned.1.call-start = ((), (), s32[]{:S(2)}) async-start(), calls=%async_computation.18 | async-start | bytes 1310720 | tf_op jit(solution)/shard_map/reduce_scatter | solution.py:308
  839.5 127.7 %copy-start.24 = (f32[64]{0:T(128)S(1)}, f32[64]{0:T(128)}, u32[]{:S(2)}) copy-start(f32[64]{0:T(128)} %copy-done.23) | copy-start | bytes 772
  971.7 197.5 %reduce-scatter.13.cloned.1.call-start = ((), (), s32[]{:S(2)}) async-start(), calls=%async_computation.19 | async-start | bytes 9732096 | tf_op jit(solution)/shard_map/reduce_scatter | solution.py:288
  974.4 46.6 %copy-start.8 = (bf16[256,2048]{1,0:T(8,128)(2,1)S(1)}, bf16[256,2048]{1,0:T(8,128)(2,1)}, u32[]{:S(2)}) copy-start(bf16[256,2048]{1,0:T(8,128)(2,1)} %param.17) | copy-start | bytes 3145732
  974.5 46.6 %copy-start.14 = (f32[1,2048]{1,0:T(1,128)S(1)}, f32[1,2048]{1,0:T(1,128)}, u32[]{:S(2)}) copy-start(f32[1,2048]{1,0:T(1,128)} %copy-done.13) | copy-start | bytes 24580
  1034.7 321.9 %reduce-scatter.15.cloned.1.call-start = ((), (), s32[]{:S(2)}) async-start(), calls=%async_computation.21 | async-start | bytes 8650752 | tf_op jit(solution)/shard_map/reduce_scatter | solution.py:288
  1051.9 465.9 %reduce-scatter.17.cloned.1.call-start = ((), (), s32[]{:S(2)}) async-start(), calls=%async_computation.23 | async-start | bytes 11796480 | tf_op jit(solution)/shard_map/reduce_scatter | solution.py:258
  1090.1 431.9 %copy-start.2 = (s32[166]{0:T(256)S(1)}, s32[166]{0:T(256)}, u32[]{:S(2)}) copy-start(s32[166]{0:T(256)} %param.20) | copy-start | bytes 1996
  1090.1 528.7 %all-gather.25.cloned.1.call-start = ((), (), s32[]{:S(2)}) async-start(), calls=%async_computation.20 | async-start | bytes 2654208 | tf_op jit(solution)/shard_map/all_gather | solution.py:289
  1169.2 449.6 %all-gather.27.cloned.1.call-start = ((), (), s32[]{:S(2)}) async-start(), calls=%async_computation.22 | async-start | bytes 2359296 | tf_op jit(solution)/shard_map/all_gather | solution.py:289
  1356.6 325.0 %all-gather.29.cloned.1.call-start = ((), (), s32[]{:S(2)}) async-start(), calls=%async_computation.24 | async-start | bytes 21233664 | tf_op jit(solution)/shard_map/all_gather | solution.py:260
  1525.1 89.2 %copy-start.17 = (f32[2,2048]{1,0:T(2,128)S(1)}, f32[2,2048]{1,0:T(2,128)}, u32[]{:S(2)}) copy-start(f32[2,2048]{1,0:T(2,128)} %param.27) | copy-start | bytes 49156
  1525.1 89.3 %copy-start.21 = (f32[2,2048]{1,0:T(2,128)S(1)}, f32[2,2048]{1,0:T(2,128)}, u32[]{:S(2)}) copy-start(f32[2,2048]{1,0:T(2,128)} %param.28) | copy-start | bytes 49156
  1525.1 89.3 %copy-start.22 = (f32[2,2048]{1,0:T(2,128)S(1)}, f32[2,2048]{1,0:T(2,128)}, u32[]{:S(2)}) copy-start(f32[2,2048]{1,0:T(2,128)} %param.29) | copy-start | bytes 49156
  1636.7 53.8 %copy-start.25 = (pred[21]{0:T(512)(128)(4,1)S(1)}, pred[21]{0:T(512)(128)(4,1)}, u32[]{:S(2)}) copy-start(pred[21]{0:T(512)(128)(4,1)} %get-tuple-element.671) | copy-start | bytes 67
  1636.7 53.8 %copy-start.26 = (pred[21]{0:T(512)(128)(4,1)S(1)}, pred[21]{0:T(512)(128)(4,1)}, u32[]{:S(2)}) copy-start(pred[21]{0:T(512)(128)(4,1)} %broadcast_compare_fusion) | copy-start | bytes 67
  (16 other events, 144.1 us)
Sparse Core Ops, SparseCore 0:
  9.9 114.7 all-gather.12
  134.5 48.3 all-gather.14
  184.8 93.1 all-gather.16
  279.9 219.8 all-gather.20
  502.1 52.5 all-gather.18
  556.5 54.3 all-gather.22
  648.1 71.2 reduce-scatter.8
  723.3 71.2 reduce-scatter.6
  971.8 35.7 reduce-scatter.10
  1034.8 134.3 reduce-scatter.12
  1171.5 185.0 reduce-scatter.14
  1358.8 158.9 reduce-scatter.16
  1519.6 30.0 all-gather.24
  1551.5 28.3 all-gather.26
  1582.2 99.3 all-gather.28
